TPU v7x, 32 devices: a whole 2x2x4 slice. The times are simulated.
32 devices in a mesh: section: 4 (over x, core), dp: 8 (over z, y).
Axes of the slice: x: 2, y: 2, z: 4, core: 2. Of those that a mesh axis runs over, the one named last changes fastest.
Arguments:
- token_ids: int32 [2, 16], P(None, 'dp'), may hold values from 0 to 8191
- target_ids: int32 [2, 16], P(None, 'dp'), may hold values from 0 to 8191
- table: bfloat16 [8192, 4608], P(('section', 'dp')), may hold values from -0.06629126 to 0.06629126
- norm_gain: bfloat16 [2, 4, 4608], P(None, 'section'), may hold values from 0.099609375 to 1.8984375
- w_in: bfloat16 [2, 4, 8, 4608], P(None, 'section'), may hold values from -0.09375 to 0.09375
- w_out: bfloat16 [2, 4, 8, 4608], P(None, 'section'), may hold values from -2 to 2
- final_gain: bfloat16 [4608], replicated, may hold values from 0.099609375 to 1.8984375
Outputs:
- token_loss: float32 [2, 16], P(None, 'dp')
- table_grad: bfloat16 [8192, 4608], P(('section', 'dp'))
All inputs are finite; a program needn't handle non-finite values.
Results may differ from a plain program's by a relative error of at most 0.013.
The roundings to bfloat16 on the way count: a program that leaves them out, or rounds other values in their place, can miss the bound.
Values may be sent and summed in bfloat16 or wider, within the bound.
A program may use at most 64 MiB of HBM per device.

v0:
```python
import math

import jax
import jax.numpy as jnp
from jax import lax
from jax.sharding import PartitionSpec as P

EPS = 1e-06
CAP = 30.0
GELU_C = 0.7978845608028654


def shifted(block, axis, distance):
    devices = range(lax.axis_size(axis))
    route = [((i - distance) % len(devices), i) for i in devices]
    return lax.ppermute(block, axis, route)


def from_root(block, axis, source):
    block = jnp.where(lax.axis_index(axis) == source, block, jnp.zeros_like(block))
    return lax.psum(block, axis)


def gelu_tanh(values):
    return 0.5 * values * (1.0 + jnp.tanh(GELU_C * (values + 0.044715 * values * values * values)))


def gelu_slope(values):
    inner = jnp.tanh(GELU_C * (values + 0.044715 * values * values * values))
    return 0.5 * (1.0 + inner) + 0.5 * values * (1.0 - inner * inner) * GELU_C * (
        1.0 + 3.0 * 0.044715 * values * values
    )


def normalize(rows_in):
    values = rows_in.astype(jnp.float32)
    scale = lax.rsqrt(jnp.mean(values * values, axis=-1, keepdims=True) + EPS)
    return (values * scale, scale)


def norm_back(normed, scale, grad):
    return scale * (grad - normed * jnp.mean(grad * normed, axis=-1, keepdims=True))


def layer_forward(rows_in, gain, first_proj, second_proj):
    normed, scale = normalize(rows_in)
    activated = (normed * gain.astype(jnp.float32)).astype(jnp.bfloat16)
    preact = lax.dot_general(
        activated, first_proj, (((1,), (1,)), ((), ())), preferred_element_type=jnp.float32
    )
    hidden = gelu_tanh(preact).astype(jnp.bfloat16)
    branch = jnp.dot(hidden, second_proj, preferred_element_type=jnp.float32)
    return (rows_in.astype(jnp.float32) + branch).astype(jnp.bfloat16)


def layer_backward(rows_in, gain, first_proj, second_proj, grad_out):
    normed, scale = normalize(rows_in)
    gain_float = gain.astype(jnp.float32)
    activated = (normed * gain_float).astype(jnp.bfloat16)
    preact = lax.dot_general(
        activated, first_proj, (((1,), (1,)), ((), ())), preferred_element_type=jnp.float32
    )
    hidden_grad = lax.dot_general(
        grad_out, second_proj, (((1,), (1,)), ((), ())), preferred_element_type=jnp.float32
    )
    preact_grad = (hidden_grad * gelu_slope(preact)).astype(jnp.bfloat16)
    act_grad = jnp.dot(preact_grad, first_proj, preferred_element_type=jnp.float32)
    return (grad_out.astype(jnp.float32) + norm_back(normed, scale, act_grad * gain_float)).astype(
        jnp.bfloat16
    )


def per_device(token_ids, target_ids, table, norm_gain, w_in, w_out, final_gain):
    sections = lax.axis_size("section")
    section_index = lax.axis_index("section")
    replicas = lax.axis_size("dp")
    replica_index = lax.axis_index("dp")
    batches, width = token_ids.shape
    rows_dev, dim = table.shape
    embed_scale = math.sqrt(dim)
    offset = (section_index * replicas + replica_index) * rows_dev
    columns = jnp.arange(rows_dev, dtype=jnp.int32)
    final_scale = final_gain.astype(jnp.float32)
    ids = lax.all_gather(jnp.concatenate([token_ids, target_ids], 0), "dp", axis=1, tiled=True)
    gains = lax.all_gather(norm_gain, "section", axis=1, tiled=True).reshape(-1, dim)
    first = lax.all_gather(w_in, "section", axis=1, tiled=True).reshape(
        2 * sections, -1, dim
    )
    second = lax.all_gather(w_out, "section", axis=1, tiled=True).reshape(
        2 * sections, -1, dim
    )
    all_inputs, all_targets = ids[:batches], ids[batches:]
    wide = all_inputs.shape[1]
    token_count = batches * wide
    chosen = ((all_inputs.reshape(token_count) - offset)[:, None] == columns[None, :]).astype(
        jnp.bfloat16
    )
    looked = jnp.dot(chosen, table, preferred_element_type=jnp.float32).astype(jnp.bfloat16)
    looked = lax.psum(looked, ("section", "dp")).astype(jnp.float32)
    rows = (looked * embed_scale).astype(jnp.bfloat16)

    def forward(rows, weights):
        return layer_forward(rows, *weights), rows

    rows, inputs = lax.scan(forward, rows, (gains, first, second))
    normed, scale = normalize(rows)
    head_input = (normed * final_scale).astype(jnp.bfloat16)
    scores = lax.dot_general(
        head_input, table, (((1,), (1,)), ((), ())), preferred_element_type=jnp.float32
    )
    squash = jnp.tanh(scores / CAP)
    capped = CAP * squash
    powers = jnp.exp(capped)
    goal_local = all_targets.reshape(token_count) - offset
    target_mask = goal_local[:, None] == columns[None, :]
    stats = lax.psum(
        jnp.stack(
            [
                jnp.sum(powers, axis=1),
                jnp.sum(jnp.where(target_mask, capped, jnp.float32(0.0)), axis=1),
            ]
        ),
        ("section", "dp"),
    )
    exp_total, target_score = stats[0], stats[1]
    loss_all = (jnp.log(exp_total) - target_score).reshape(batches, wide)
    token_loss = lax.dynamic_slice_in_dim(loss_all, replica_index * width, width, 1)
    score_grad = (
        (powers / exp_total[:, None] - target_mask.astype(jnp.float32)) * (1.0 - squash * squash)
    ).astype(jnp.bfloat16)
    partial_value = jnp.dot(score_grad, table, preferred_element_type=jnp.float32)
    head_in_grad = lax.psum(partial_value, ("section", "dp"))
    grad = norm_back(normed, scale, head_in_grad * final_scale).astype(jnp.bfloat16)

    def backward(grad, saved):
        return layer_backward(*saved, grad), None

    grad, _ = lax.scan(backward, grad, (inputs, gains, first, second), reverse=True)
    head_grad = lax.dot_general(
        score_grad, head_input, (((0,), (0,)), ((), ())), preferred_element_type=jnp.float32
    )
    embed_grad = (
        lax.dot_general(chosen, grad, (((0,), (0,)), ((), ())), preferred_element_type=jnp.float32)
        * embed_scale
    )
    return (token_loss, (head_grad + embed_grad).astype(jnp.bfloat16))


def solution(mesh):
    return jax.shard_map(
        per_device,
        mesh=mesh,
        in_specs=(
            P(None, "dp"),
            P(None, "dp"),
            P(("section", "dp"), None),
            P(None, "section", None),
            P(None, "section", None, None),
            P(None, "section", None, None),
            P(),
        ),
        out_specs=(P(None, "dp"), P(("section", "dp"), None)),
        check_vma=False,
    )
```

profile of v0, /device:TPU:0, one launch (start us, length us, event | category | flops | bytes accessed | tf_op | source)
XLA Modules:
  0.0 419.9 jit_solution(2897440791546498494)
XLA Ops:
  8.2 22.3 %all-gather = s32[8,2,4]{2,1,0:T(2,128)S(1)} all-gather(s32[1,2,4]{2,1,0:T(2,128)S(1)} %bitcast.102), channel_id=1, replica_groups=mesh['section'=4,'dp'=8] {'dp'}, dimensions={0}, use_global_device_ids=true | all-gather | bytes 288 | tf_op jit(solution)/shard_map/all_gather | solution.py:84
  32.1 5.3 %all_gather.13 = bf16[2,4,4608]{2,0,1:T(2,128)(2,1)S(1)} all-gather(bf16[2,1,4608]{2,0,1:T(2,128)(2,1)S(1)} %copy-done.3), channel_id=1, replica_groups=mesh['section'=4,'dp'=8] {'section'}, dimensions={1}, use_global_device_ids=true | all-gather | bytes 92160 | tf_op jit(solution)/shard_map/all_gather | solution.py:85
  38.0 8.2 %all_gather.14 = bf16[2,4,8,4608]{3,2,1,0:T(8,128)(2,1)} all-gather(bf16[2,1,8,4608]{3,2,1,0:T(8,128)(2,1)S(1)} %copy-done.1), channel_id=1, replica_groups=mesh['section'=4,'dp'=8] {'section'}, dimensions={1}, use_global_device_ids=true | all-gather | bytes 737280 | tf_op jit(solution)/shard_map/all_gather | solution.py:86
  46.2 8.1 %all_gather.15 = bf16[2,4,8,4608]{3,2,1,0:T(8,128)(2,1)} all-gather(bf16[2,1,8,4608]{3,2,1,0:T(8,128)(2,1)S(1)} %copy-done.2), channel_id=1, replica_groups=mesh['section'=4,'dp'=8] {'section'}, dimensions={1}, use_global_device_ids=true | all-gather | bytes 737280 | tf_op jit(solution)/shard_map/all_gather | solution.py:89
  54.3 100.7 %all-reduce.3.cloned.1.call-done = bf16[32,4608]{1,0:T(8,128)(2,1)} async-done(((bf16[32,4608]{1,0:T(8,128)(2,1)}), bf16[32,4608]{1,0:T(8,128)(2,1)}) %all-reduce.3.cloned.1.call-update) | async-done | bytes 294928 | tf_op jit(solution)/shard_map/psum | solution.py:99
  156.0 28.2 %while.26 = (s32[]{:T(128)}, bf16[32,4608]{1,0:T(8,128)(2,1)S(1)}, bf16[8,32,4608]{2,1,0:T(8,128)(2,1)}, bf16[8,4608]{1,0:T(8,128)(2,1)}, bf16[8,8,4608]{2,1,0:T...) while((s32[]{:T(128)}, bf16[32,4608]{1,0:T(8,128)(2,1)S(1)}, bf16[8,32,4608]{2,1,0:T(8,128)(2,1)}, ...), condition=%wide.region_3.4_spmd, body=%wide.region_1.3_spmd.sunk | while | flops 6200098 | bytes 2556893 | solution.py:105
  161.5 1.6 fusion.132
  165.0 1.6 fusion.132
  168.5 1.6 fusion.132
  175.6 1.6 fusion.132
  179.1 1.6 fusion.132
  185.4 41.2 %psum.22 = f32[2,32]{1,0:T(2,128)S(1)} all-reduce(f32[2,32]{1,0:T(2,128)S(1)} %pad_maximum_fusion), channel_id=1, replica_groups=mesh['section'=4,'dp'=8] {'section','dp'}, use_global_device_ids=true, to_apply=%region_7.8 | all-reduce | flops 64 | bytes 512 | tf_op jit(solution)/shard_map/psum | solution.py:116
  228.8 3.0 fusion.102
  231.8 123.7 %all-reduce.5.cloned.1.call-done = f32[32,4608]{1,0:T(8,128)} async-done(((f32[32,4608]{1,0:T(8,128)}), f32[32,4608]{1,0:T(8,128)}) %all-reduce.5.cloned.1.call-update) | async-done | bytes 589840 | tf_op jit(solution)/shard_map/psum | solution.py:132
  358.0 50.4 %while.27 = (s32[]{:T(128)}, bf16[32,4608]{1,0:T(8,128)(2,1)S(1)}, bf16[8,32,4608]{2,1,0:T(8,128)(2,1)}, bf16[8,8,4608]{2,1,0:T(8,128)(2,1)}, bf16[8,4608]{1,0:T...) while((s32[]{:T(128)}, bf16[32,4608]{1,0:T(8,128)(2,1)S(1)}, ...), condition=%wide.region_13.14_spmd, body=%wide.region_10.13_spmd.sunk | while | flops 10036515 | bytes 3535725 | solution.py:138
  361.4 1.7 fusion.139
  367.7 1.7 fusion.139
  374.0 1.7 fusion.139
  380.3 1.7 fusion.139
  386.6 1.7 fusion.139
  392.9 1.7 fusion.139
  399.1 1.7 fusion.139
  405.4 1.7 fusion.139
  408.4 4.6 %fusion.91 = bf16[256,4608]{1,0:T(8,128)(2,1)} fusion(f32[256,4608]{1,0:T(8,128)} %fusion.102, bf16[32,4608]{1,0:T(8,128)(2,1)S(1)} %get-tuple-element.159, s32[32]{0:T(128)S(1)} %sub.70), kind=kOutput, calls=%fused_computation.92 | convolution fusion | flops 79044608 | bytes 7372928 | tf_op jit(solution)/shard_map/dot_general | solution.py:143
  (128 shorter events, 66.2 us)
Async XLA Ops:
  7.2 23.5 %copy-start = (bf16[256,4608]{1,0:T(8,128)(2,1)S(1)}, bf16[256,4608]{1,0:T(8,128)(2,1)}, u32[]{:S(2)}) copy-start(bf16[256,4608]{1,0:T(8,128)(2,1)} %param.13) | copy-start | bytes 7077892
  7.2 24.9 %copy-start.4 = (bf16[4608]{0:T(1024)(128)(2,1)S(1)}, bf16[4608]{0:T(1024)(128)(2,1)}, u32[]{:S(2)}) copy-start(bf16[4608]{0:T(1024)(128)(2,1)} %param.17) | copy-start | bytes 27652
  7.2 24.9 %copy-start.3 = (bf16[2,1,4608]{2,0,1:T(2,128)(2,1)S(1)}, bf16[2,1,4608]{2,0,1:T(2,128)(2,1)}, u32[]{:S(2)}) copy-start(bf16[2,1,4608]{2,0,1:T(2,128)(2,1)} %param.14) | copy-start | bytes 55300
  7.2 30.8 %copy-start.1 = (bf16[2,1,8,4608]{3,2,1,0:T(8,128)(2,1)S(1)}, bf16[2,1,8,4608]{3,2,1,0:T(8,128)(2,1)}, u32[]{:S(2)}) copy-start(bf16[2,1,8,4608]{3,2,1,0:T(8,128)(2,1)} %param.15) | copy-start | bytes 442372
  7.2 39.0 %copy-start.2 = (bf16[2,1,8,4608]{3,2,1,0:T(8,128)(2,1)S(1)}, bf16[2,1,8,4608]{3,2,1,0:T(8,128)(2,1)}, u32[]{:S(2)}) copy-start(bf16[2,1,8,4608]{3,2,1,0:T(8,128)(2,1)} %param.16) | copy-start | bytes 442372
  7.2 147.8 %all-reduce.3.cloned.1.call-start = ((), (), s32[]{:S(2)}) async-start(), calls=%async_computation | async-start | bytes 589824 | tf_op jit(solution)/shard_map/psum | solution.py:99
  31.9 323.5 %all-reduce.5.cloned.1.call-start = ((), (), s32[]{:S(2)}) async-start(), calls=%async_computation.1 | async-start | bytes 1179648 | tf_op jit(solution)/shard_map/psum | solution.py:132
Sparse Core Ops, SparseCore 0:
  32.0 122.9 all-reduce.2
  228.3 127.1 all-reduce.4
where the time goes:
time: 422 us; the launch traced here: 420 us
  waiting for transfers between devices  224 us (53%)
  blocking collectives  85 us (20%)
  matrix products  47.9 us (11%)
  other arithmetic  40 us (9%)
  between operations  14.1 us (3%)
  local copies, waits for them, and re-layouts  7.85 us (2%)
    psum x1, waiting for transfers between devices, per_device(): head_in_grad = lax.psum(partial_value, ('section', 'dp'))  124 us
    psum x1, waiting for transfers between devices, per_device(): looked = lax.psum(looked, ('section', 'dp')).astype(jnp.float32)  101 us
    psum x1, blocking collectives, per_device(): lax.psum(jnp.stack([jnp.sum(powers, axis=1), jnp.sum(jnp.where(target_mas...  41.2 us
    all_gather x1, blocking collectives, per_device(): lax.all_gather(jnp.concatenate([token_ids, target_ids], 0), 'dp', axis=1,...  22.3 us
    dot_general x8, matrix products, layer_backward(): jnp.dot(preact_grad, first_proj, preferred_element_type=jnp.float32)  14 us
    dot_general x8, matrix products, layer_forward(): branch = jnp.dot(hidden, second_proj, preferred_element_type=jnp.float32)  12.8 us
    reduce_sum x17, other arithmetic, normalize(): scale = lax.rsqrt(jnp.mean(values * values, axis=-1, keepdims=True) + EPS)  10.7 us
    dot_general x8, matrix products, layer_backward(): lax.dot_general(activated, first_proj, (((1,), (1,)), ((), ())), preferre...  9.88 us
  transfers between devices with their start and end apart: 2, of which 2 were waited for; matrix products, arithmetic and copies ran while one was open for 1% of the time, Pallas kernels for 0%

commit v1 on v0

v1 whole, which is shorter than its diff:
```python
import functools
import math

import jax
import jax.numpy as jnp
from jax import lax
from jax.experimental import pallas as pl
from jax.experimental.pallas import tpu as pltpu
from jax.sharding import PartitionSpec as P

EPS = 1e-06
CAP = 30.0
GELU_C = 0.7978845608028654
LANES = 128
F32 = jnp.float32
BF16 = jnp.bfloat16
IDS, GAIN, WIN, WOUT, LOOK, HEAD, STAT, GRAD, EMB = range(9)


def gelu_tanh(values):
    return 0.5 * values * (1.0 + jnp.tanh(GELU_C * (values + 0.044715 * values * values * values)))


def gelu_slope(values):
    inner = jnp.tanh(GELU_C * (values + 0.044715 * values * values * values))
    return 0.5 * (1.0 + inner) + 0.5 * values * (1.0 - inner * inner) * GELU_C * (
        1.0 + 3.0 * 0.044715 * values * values
    )


def rounded(values):
    return values.astype(BF16).astype(F32)


def cascade(
    sections, replicas, per_dp, pad,
    ids_ref, table_ref, gain_ref, win_ref, wout_ref, fgain_ref,
    loss_ref, sg_ref, chosen_ref, head_ref, emb_ref,
    idbuf, idrow, gains, wins, wouts, flat, look_out, look_in, tok, layer_in,
    head_out, head_in, stat_out, stat_in, grad_out, grad_in, emb_out, emb_in,
    send_sem, recv_sem,
):
    devices = sections * replicas
    tokens = replicas * per_dp
    rows_dev, dim = table_ref.shape
    chunks = dim // LANES
    layers = 2 * sections
    scale_in = math.sqrt(dim)
    sec, rep = lax.axis_index("section"), lax.axis_index("dp")
    me = sec * replicas + rep
    offset = me * rows_dev
    all_own = per_dp == sections
    own = sec < per_dp
    my_token = rep * per_dp + sec if all_own else jnp.where(own, rep * per_dp + sec, -1)

    def if_own(body):
        if all_own:
            body()
        else:
            pl.when(own)(body)

    def spread(phase, count, first, target, skip, src, dst):
        def step(i, _):
            at = lax.rem(first + i, count)

            @pl.when(at != skip)
            def _():
                pltpu.make_async_remote_copy(
                    src_ref=src(at),
                    dst_ref=dst,
                    send_sem=send_sem.at[phase],
                    recv_sem=recv_sem.at[phase],
                    device_id=target(at),
                    device_id_type=pl.DeviceIdType.MESH,
                ).start()

            @pl.when(at == skip)
            def _():
                pltpu.make_async_copy(src(at), dst, recv_sem.at[phase]).start()

            return 0

        lax.fori_loop(0, count, step, 0)

    def take(ref, sem):
        pltpu.make_async_copy(ref, ref, sem).wait()

    def any_device(n):
        return (n // replicas, n % replicas)

    def token_device(t):
        return (t % per_dp, t // per_dp)

    barrier = pltpu.get_barrier_semaphore()

    def greet(i, _):
        n = lax.rem(me + 1 + i, devices)
        pl.semaphore_signal(
            barrier, inc=1, device_id=any_device(n), device_id_type=pl.DeviceIdType.MESH
        )
        return 0

    lax.fori_loop(0, devices - 1, greet, 0)
    flat[...] = jnp.zeros_like(flat)
    tok[...] = jnp.zeros_like(tok)
    pl.semaphore_wait(barrier, devices - 1)

    spread(IDS, replicas, rep, lambda d: (sec, d), rep, lambda d: ids_ref, idbuf.at[rep])
    for phase, src, dst in ((GAIN, gain_ref, gains), (WIN, win_ref, wins), (WOUT, wout_ref, wouts)):
        spread(
            phase, sections, sec, lambda s: (s, rep), sec, lambda s, src=src: src, dst.at[sec]
        )

    take(idbuf, recv_sem.at[IDS])
    for d in range(replicas):
        for kind in range(2):
            for k in range(per_dp):
                idrow[kind, pl.ds(d * per_dp + k, 1), :] = idbuf[
                    d, pl.ds(kind * per_dp + k, 1), :
                ]
    wide = lambda value: jnp.concatenate([value] * (rows_dev // LANES), axis=1)
    column = lax.broadcasted_iota(jnp.int32, (tokens, rows_dev), 1) + offset
    chosen = jnp.where(wide(idrow[0]) == column, 1.0, 0.0).astype(BF16)
    mask = wide(idrow[1]) == column
    chosen_ref[...] = chosen

    def scatter(left, phase, out, into):
        for j in range(0, chunks, 2):
            part = jnp.dot(
                left, table_ref[:, j * LANES : (j + 2) * LANES], preferred_element_type=F32
            )
            flat[pl.ds(j, tokens, stride=pad), :] = part[:, :LANES]
            flat[pl.ds(j + 1, tokens, stride=pad), :] = part[:, LANES:]
        out[...] = flat[...].astype(BF16).reshape(tokens, pad, LANES)
        spread(
            phase, tokens, rep * per_dp + sec, token_device, my_token,
            lambda t: out.at[t], into.at[me],
        )

    def total(into):
        return lax.fori_loop(
            0, devices, lambda n, acc: acc + into[n].astype(F32), jnp.zeros((pad, LANES), F32)
        )

    def spread_rows(values):
        tok[...] = values
        return jnp.concatenate(
            [jnp.broadcast_to(tok[j : j + 1, :], (8, LANES)) for j in range(chunks)], axis=1
        )

    def pack_row(values, out):
        for j in range(chunks):
            tok[j : j + 1, :] = values[0:1, j * LANES : (j + 1) * LANES]
        out[...] = tok[...].astype(BF16)

    def norm(x):
        scale = lax.rsqrt(jnp.sum(x * x, axis=1, keepdims=True) * (1.0 / dim) + EPS)
        return x * scale, scale

    def weights(layer):
        s, c = layer % sections, layer // sections
        return (
            spread_rows(gains[s, c].astype(F32)),
            wins[s, c].astype(F32),
            wouts[s, c].astype(F32),
        )

    def gather(phase, block, into):
        if_own(
            lambda: spread(
                phase, devices, me, any_device, me, lambda n: block, into.at[my_token]
            )
        )

    def unpack(into, out):
        flat[...] = into[...].reshape(tokens * pad, LANES).astype(F32)
        for j in range(chunks):
            out[:, j * LANES : (j + 1) * LANES] = flat[
                pl.ds(j, tokens, stride=pad), :
            ].astype(BF16)

    scatter(chosen, LOOK, look_out, look_in)
    take(gains, recv_sem.at[GAIN])
    take(wins, recv_sem.at[WIN])
    take(wouts, recv_sem.at[WOUT])

    def forward():
        take(look_in, recv_sem.at[LOOK])
        x = spread_rows(rounded(total(look_in) * scale_in))

        def layer(index, x):
            layer_in[index] = x
            gain, first, second = weights(index)
            normed, _ = norm(x)
            pre = jnp.sum(rounded(normed * gain) * first, axis=1, keepdims=True)
            hidden = rounded(gelu_tanh(pre))
            return rounded(x + jnp.sum(hidden * second, axis=0, keepdims=True))

        x = lax.fori_loop(0, layers, layer, x)
        layer_in[layers] = x
        normed, _ = norm(x)
        pack_row(normed * spread_rows(fgain_ref[...].astype(F32)), head_out)

    if_own(forward)
    gather(HEAD, head_out, head_in)
    take(head_in, recv_sem.at[HEAD])
    unpack(head_in, head_ref)

    scores = lax.dot_general(
        head_ref[...], table_ref[...], (((1,), (1,)), ((), ())), preferred_element_type=F32
    )
    squash = jnp.tanh(scores / CAP)
    capped = CAP * squash
    powers = jnp.exp(capped)
    exp_sum = jnp.sum(powers, axis=1, keepdims=True)
    goal = jnp.sum(jnp.where(mask, capped, 0.0), axis=1, keepdims=True)
    groups = tokens // 8
    lane = lax.broadcasted_iota(jnp.int32, (8, LANES), 1)
    tile = jnp.zeros((8, LANES), F32)
    for g in range(groups):
        tile = jnp.where(lane == g, exp_sum[8 * g : 8 * g + 8], tile)
        tile = jnp.where(lane == groups + g, goal[8 * g : 8 * g + 8], tile)
    stat_out[...] = tile
    spread(STAT, devices, me, any_device, me, lambda n: stat_out, stat_in.at[me])
    take(stat_in, recv_sem.at[STAT])
    tile = lax.fori_loop(
        0, devices, lambda n, acc: acc + stat_in[n], jnp.zeros((8, LANES), F32)
    )

    def column_of(first):
        return jnp.concatenate(
            [
                jnp.broadcast_to(tile[:, first + g : first + g + 1], (8, LANES))
                for g in range(groups)
            ],
            axis=0,
        )

    exp_total = column_of(0)
    loss_ref[...] = jnp.log(exp_total) - column_of(groups)
    score_grad = (
        (powers / wide(exp_total) - jnp.where(mask, 1.0, 0.0)) * (1.0 - squash * squash)
    ).astype(BF16)
    sg_ref[...] = score_grad
    scatter(score_grad, GRAD, grad_out, grad_in)

    def backward():
        take(grad_in, recv_sem.at[GRAD])
        grad = spread_rows(total(grad_in)) * spread_rows(fgain_ref[...].astype(F32))

        def back(normed, scale, grad):
            mean = jnp.sum(grad * normed, axis=1, keepdims=True) * (1.0 / dim)
            return scale * (grad - normed * mean)

        dy = rounded(back(*norm(layer_in[layers]), grad))

        def layer(step, dy):
            index = layers - 1 - step
            gain, first, second = weights(index)
            normed, scale = norm(layer_in[index])
            pre = jnp.sum(rounded(normed * gain) * first, axis=1, keepdims=True)
            hidden_grad = jnp.sum(dy * second, axis=1, keepdims=True)
            pre_grad = rounded(hidden_grad * gelu_slope(pre))
            act_grad = jnp.sum(pre_grad * first, axis=0, keepdims=True)
            return rounded(dy + back(normed, scale, act_grad * gain))

        pack_row(lax.fori_loop(0, layers, layer, dy), emb_out)

    if_own(backward)
    gather(EMB, emb_out, emb_in)
    take(emb_in, recv_sem.at[EMB])
    unpack(emb_in, emb_ref)

    take(idbuf.at[pl.ds(0, replicas - 1)], send_sem.at[IDS])
    for phase, buf in ((GAIN, gains), (WIN, wins), (WOUT, wouts)):
        take(buf.at[pl.ds(0, sections - 1)], send_sem.at[phase])
    take(stat_in.at[pl.ds(0, devices - 1)], send_sem.at[STAT])

    def owned():
        take(look_out.at[pl.ds(0, tokens - 1)], send_sem.at[LOOK])
        take(grad_out.at[pl.ds(0, tokens - 1)], send_sem.at[GRAD])
        take(look_in.at[pl.ds(0, devices - 1)], send_sem.at[HEAD])
        take(grad_in.at[pl.ds(0, devices - 1)], send_sem.at[EMB])

    if_own(owned)
    if not all_own:

        @pl.when(jnp.logical_not(own))
        def _():
            take(look_out, send_sem.at[LOOK])
            take(grad_out, send_sem.at[GRAD])


def table_kernel(scale, sg_ref, chosen_ref, head_ref, emb_ref, out_ref):
    over = (((0,), (0,)), ((), ()))
    head = lax.dot_general(sg_ref[...], head_ref[...], over, preferred_element_type=F32)
    emb = lax.dot_general(chosen_ref[...], emb_ref[...], over, preferred_element_type=F32)
    out_ref[...] = (head + emb * scale).astype(BF16)


def per_device(token_ids, target_ids, table, norm_gain, w_in, w_out, final_gain):
    sections, replicas = lax.axis_size("section"), lax.axis_size("dp")
    batches, width = token_ids.shape
    rows_dev, dim = table.shape
    rank = w_in.shape[2]
    per_dp = batches * width
    tokens = replicas * per_dp
    devices = sections * replicas
    chunks = dim // LANES
    pad = (chunks + 15) // 16 * 16
    assert per_dp <= sections and tokens % 8 == 0
    assert chunks % 2 == 0 and rows_dev % LANES == 0
    ids = jnp.concatenate([token_ids.reshape(per_dp), target_ids.reshape(per_dp)])
    ids = jnp.broadcast_to(ids[:, None], (2 * per_dp, LANES))
    fill = lambda rows: jnp.pad(
        rows.reshape(rows.shape[:-1] + (chunks, LANES)),
        ((0, 0),) * (rows.ndim - 1) + ((0, pad - chunks), (0, 0)),
    )
    block = (pad, LANES)
    vmem = pl.BlockSpec(memory_space=pltpu.VMEM)
    loss, score_grad, chosen, head, emb = pl.pallas_call(
        functools.partial(cascade, sections, replicas, per_dp, pad),
        out_shape=(
            jax.ShapeDtypeStruct((tokens, LANES), F32),
            jax.ShapeDtypeStruct((tokens, rows_dev), BF16),
            jax.ShapeDtypeStruct((tokens, rows_dev), BF16),
            jax.ShapeDtypeStruct((tokens, dim), BF16),
            jax.ShapeDtypeStruct((tokens, dim), BF16),
        ),
        in_specs=[vmem] * 6,
        out_specs=(vmem,) * 5,
        scratch_shapes=[
            pltpu.VMEM((replicas, 2 * per_dp, LANES), jnp.int32),
            pltpu.VMEM((2, tokens, LANES), jnp.int32),
            pltpu.VMEM((sections, 2) + block, BF16),
            pltpu.VMEM((sections, 2, rank, dim), BF16),
            pltpu.VMEM((sections, 2, rank, dim), BF16),
            pltpu.VMEM((tokens * pad, LANES), F32),
            pltpu.VMEM((tokens,) + block, BF16),
            pltpu.VMEM((devices,) + block, BF16),
            pltpu.VMEM(block, F32),
            pltpu.VMEM((2 * sections + 1, 8, dim), F32),
            pltpu.VMEM(block, BF16),
            pltpu.VMEM((tokens,) + block, BF16),
            pltpu.VMEM((8, LANES), F32),
            pltpu.VMEM((devices, 8, LANES), F32),
            pltpu.VMEM((tokens,) + block, BF16),
            pltpu.VMEM((devices,) + block, BF16),
            pltpu.VMEM(block, BF16),
            pltpu.VMEM((tokens,) + block, BF16),
            pltpu.SemaphoreType.DMA((9,)),
            pltpu.SemaphoreType.DMA((9,)),
        ],
        compiler_params=pltpu.CompilerParams(
            collective_id=0, has_side_effects=True, vmem_limit_bytes=52 << 20
        ),
        name="cascade",
    )(ids, table, fill(norm_gain[:, 0]), w_in[:, 0], w_out[:, 0], fill(final_gain))
    step = 512
    full = pl.BlockSpec((tokens, rows_dev), lambda i: (0, 0))
    piece = pl.BlockSpec((tokens, step), lambda i: (0, i))
    table_grad = pl.pallas_call(
        functools.partial(table_kernel, math.sqrt(dim)),
        out_shape=jax.ShapeDtypeStruct((rows_dev, dim), BF16),
        grid=(dim // step,),
        in_specs=[full, full, piece, piece],
        out_specs=pl.BlockSpec((rows_dev, step), lambda i: (0, i)),
        name="table_grad",
    )(score_grad, chosen, head, emb)
    token_loss = lax.dynamic_slice_in_dim(
        loss[:, 0], lax.axis_index("dp") * per_dp, per_dp, 0
    ).reshape(batches, width)
    return (token_loss, table_grad)


def solution(mesh):
    return jax.shard_map(
        per_device,
        mesh=mesh,
        in_specs=(
            P(None, "dp"),
            P(None, "dp"),
            P(("section", "dp"), None),
            P(None, "section", None),
            P(None, "section", None, None),
            P(None, "section", None, None),
            P(),
        ),
        out_specs=(P(None, "dp"), P(("section", "dp"), None)),
        check_vma=False,
    )
```

time: 422 us -> 90.3 us (0.21)
  waiting for transfers between devices: 224 us -> 0 us
  blocking collectives: 85 us -> 0 us
  Pallas kernels: 0 us -> 80.4 us
  matrix products: 47.9 us -> 0 us
  other arithmetic: 40 us -> 0.08 us
  between operations: 14.1 us -> 0.67 us
    psum x2 -> x0, waiting for transfers between devices: 224 us -> none  [the longest x1 124 us: per_device(): head_in_grad = lax.psum(partial_value, ('section', 'dp'))]
    pallas_call x0 -> x2, Pallas kernels: none -> 80.4 us  [the longest x1 73.8 us: per_device(): pl.pallas_call(functools.partial(cascade, sections, replicas, per_dp, pad...]
    dot_general x29 -> x0, matrix products: 47.9 us -> none  [the longest x8 14 us: layer_backward(): jnp.dot(preact_grad, first_proj, preferred_element_type=jnp.float32)]
    all_gather x4 -> x0, blocking collectives: 43.8 us -> none  [the longest x1 22.3 us: per_device(): lax.all_gather(jnp.concatenate([token_ids, target_ids], 0), 'dp', axis=1,...]
    psum x1 -> x0, blocking collectives: 41.2 us -> none  [per_device(): lax.psum(jnp.stack([jnp.sum(powers, axis=1), jnp.sum(jnp.where(target_mas...]
    mul x16 -> x0, other arithmetic: 15.2 us -> none  [the longest x8 7.64 us: layer_backward(): activated = (normed * gain_float).astype(jnp.bfloat16)]
    reduce_sum x18 -> x0, other arithmetic: 12 us -> none  [the longest x17 10.7 us: normalize(): scale = lax.rsqrt(jnp.mean(values * values, axis=-1, keepdims=True) + EPS)]
    convert_element_type x11 -> x0, other arithmetic: 11.7 us -> none  [the longest x8 9.45 us: layer_backward(): (grad_out.astype(jnp.float32) + norm_back(normed, scale, act_grad * gain_...]
  transfers between devices with their start and end apart: 2 -> 0, of which waited for: 2 -> 0; matrix products, arithmetic and copies ran while one was open for 1% -> 0% of each run, Pallas kernels for 0% -> 0%
where the time goes in v1:
time: 90.3 us; the launch traced here: 89.4 us
  Pallas kernels  80.4 us (89%)
  local copies, waits for them, and re-layouts  8.24 us (9%)
    pallas_call x1, Pallas kernels, per_device(): pl.pallas_call(functools.partial(cascade, sections, replicas, per_dp, pad...  73.8 us
    pallas_call x1, Pallas kernels, per_device(): pl.pallas_call(functools.partial(table_kernel, math.sqrt(dim)), out_shape...  6.66 us
    unnamed x12, local copies, waits for them, and re-layouts  4.43 us

profile of v1, /device:TPU:0, one launch (start us, length us, event | category | flops | bytes accessed | tf_op | source)
XLA Modules:
  0.0 89.4 jit_solution(17949073046035402260)
XLA Ops:
  0.6 0.8 reshape.19
  1.4 0.8 reshape.20
  2.2 0.1 pad_add_fusion
  2.2 0.1 broadcast_in_dim.2.ids_ref
  2.3 0.7 pad.9.fgain_ref
  3.0 0.7 reshape_squeeze.3
  3.8 0.0 copy-start.2
  3.8 0.9 %copy-done.2 = bf16[2,1,8,4608]{3,2,1,0:T(8,128)(2,1)S(1)} copy-done((bf16[2,1,8,4608]{3,2,1,0:T(8,128)(2,1)S(1)}, bf16[2,1,8,4608]{3,2,1,0:T(8,128)(2,1)}, u32[]{:S(2)}) %copy-start.2) | copy-done | bytes 147480
  4.7 0.0 copy-start.3
  4.7 0.9 %copy-done.3 = bf16[2,1,8,4608]{3,2,1,0:T(8,128)(2,1)S(1)} copy-done((bf16[2,1,8,4608]{3,2,1,0:T(8,128)(2,1)S(1)}, bf16[2,1,8,4608]{3,2,1,0:T(8,128)(2,1)}, u32[]{:S(2)}) %copy-start.3) | copy-done | bytes 147480
  5.6 73.8 %cascade.1 = (f32[32,128]{1,0:T(8,128)S(1)}, bf16[32,256]{1,0:T(8,128)(2,1)S(1)}, bf16[32,256]{1,0:T(8,128)(2,1)S(1)}, bf16[32,4608]{1,0:T(8,128)(2,1)S(1)}, bf16[32,4608]{1,0:T(8,128)(2,1)S(1)}) custom-call(s32[8,128]{1,0:T(8,128)S(1)} %broadcast_in_dim.2.ids_ref, bf16[256,4608]{1,0:T(8,128)(2,1)} %table_ref.1, bf16[2,48,128]{2,1,0:T(8,128)(2,1)S(1)} %pad.8.gain_ref, ...), custom_call_target="tpu_custom_call" | custom-call | tf_op jit(solution)/shard_map/cascade/pallas_call | solution.py:321
  79.4 0.0 copy-start
  79.4 0.7 copy-done
  80.1 0.0 copy-start.1
  80.1 0.7 copy-done.1
  80.8 0.0 copy-start.4
  80.8 0.6 copy-done.4
  81.4 0.0 copy-start.5
  81.4 0.6 copy-done.5
  82.0 0.1 dynamic-slice_reduce_fusion
  82.1 0.6 reshape.22
  82.8 6.7 %table_grad.1 = bf16[256,4608]{1,0:T(8,128)(2,1)} custom-call(bf16[32,256]{1,0:T(8,128)(2,1)} %copy-done.4, bf16[32,256]{1,0:T(8,128)(2,1)} %copy-done.5, bf16[32,4608]{1,0:T(8,128)(2,1)} %copy-done, bf16[32,4608]{1,0:T(8,128)(2,1)} %copy-done.1), custom_call_target="tpu_custom_call" | custom-call | tf_op jit(solution)/shard_map/table_grad/pallas_call | solution.py:362
  (1 shorter events, 0.0 us)
Async XLA Ops:
  3.8 0.9 %copy-start.2 = (bf16[2,1,8,4608]{3,2,1,0:T(8,128)(2,1)S(1)}, bf16[2,1,8,4608]{3,2,1,0:T(8,128)(2,1)}, u32[]{:S(2)}) copy-start(bf16[2,1,8,4608]{3,2,1,0:T(8,128)(2,1)} %param.11) | copy-start | bytes 442372
  4.7 0.9 %copy-start.3 = (bf16[2,1,8,4608]{3,2,1,0:T(8,128)(2,1)S(1)}, bf16[2,1,8,4608]{3,2,1,0:T(8,128)(2,1)}, u32[]{:S(2)}) copy-start(bf16[2,1,8,4608]{3,2,1,0:T(8,128)(2,1)} %param.12) | copy-start | bytes 442372
  79.4 0.7 copy-start
  80.1 0.7 copy-start.1
  80.8 0.6 copy-start.4
  81.4 0.6 copy-start.5

commit v2 on v1

--- a/solution.py
+++ b/solution.py
@@ -14,7 +14,9 @@
 LANES = 128
 F32 = jnp.float32
 BF16 = jnp.bfloat16
-IDS, GAIN, WIN, WOUT, LOOK, HEAD, STAT, GRAD, EMB = range(9)
+IDS, LOOK, HEAD, STAT, GRAD, EMB, GAIN, WIN, WOUT = range(9)
+RELAY = 3
+TABLE = 12
 
 
 def gelu_tanh(values):
@@ -34,16 +36,17 @@
 
 def cascade(
     sections, replicas, per_dp, pad,
-    ids_ref, table_ref, gain_ref, win_ref, wout_ref, fgain_ref,
-    loss_ref, sg_ref, chosen_ref, head_ref, emb_ref,
+    ids_ref, table_hbm, gain_ref, win_ref, wout_ref,
+    loss_ref, left_ref, right_ref,
     idbuf, idrow, gains, wins, wouts, flat, look_out, look_in, tok, layer_in,
     head_out, head_in, stat_out, stat_in, grad_out, grad_in, emb_out, emb_in,
-    send_sem, recv_sem,
+    table_ref, gain_wide, kept, send_sem, recv_sem,
 ):
     devices = sections * replicas
     tokens = replicas * per_dp
     rows_dev, dim = table_ref.shape
     chunks = dim // LANES
+    head_ref = right_ref.at[pl.ds(0, tokens)]
     layers = 2 * sections
     scale_in = math.sqrt(dim)
     sec, rep = lax.axis_index("section"), lax.axis_index("dp")
@@ -80,7 +83,7 @@
 
             return 0
 
-        lax.fori_loop(0, count, step, 0)
+        lax.fori_loop(0, count, step, 0, unroll=4)
 
     def take(ref, sem):
         pltpu.make_async_copy(ref, ref, sem).wait()
@@ -91,6 +94,8 @@
     def token_device(t):
         return (t % per_dp, t // per_dp)
 
+    load = pltpu.make_async_copy(table_hbm, table_ref, recv_sem.at[TABLE])
+    load.start()
     barrier = pltpu.get_barrier_semaphore()
 
     def greet(i, _):
@@ -106,10 +111,21 @@
     pl.semaphore_wait(barrier, devices - 1)
 
     spread(IDS, replicas, rep, lambda d: (sec, d), rep, lambda d: ids_ref, idbuf.at[rep])
-    for phase, src, dst in ((GAIN, gain_ref, gains), (WIN, win_ref, wins), (WOUT, wout_ref, wouts)):
-        spread(
-            phase, sections, sec, lambda s: (s, rep), sec, lambda s, src=src: src, dst.at[sec]
-        )
+    half = sections // 2
+    side, partner = sec % 2, sec + 1 - 2 * (sec % 2)
+    stores = ((GAIN, gain_ref, gains), (WIN, win_ref, wins), (WOUT, wout_ref, wouts))
+    for phase, src, dst in stores:
+        for i in range(1, half):
+            pair = lax.rem(sec // 2 + i, half)
+            pltpu.make_async_remote_copy(
+                src_ref=src,
+                dst_ref=dst.at[side, sec // 2],
+                send_sem=send_sem.at[phase],
+                recv_sem=recv_sem.at[phase],
+                device_id=(2 * pair + side, rep),
+                device_id_type=pl.DeviceIdType.MESH,
+            ).start()
+        pltpu.make_async_copy(src, dst.at[side, sec // 2], recv_sem.at[phase]).start()
 
     take(idbuf, recv_sem.at[IDS])
     for d in range(replicas):
@@ -122,7 +138,9 @@
     column = lax.broadcasted_iota(jnp.int32, (tokens, rows_dev), 1) + offset
     chosen = jnp.where(wide(idrow[0]) == column, 1.0, 0.0).astype(BF16)
     mask = wide(idrow[1]) == column
-    chosen_ref[...] = chosen
+    left_ref[pl.ds(tokens, tokens), :] = chosen
+    left_ref[pl.ds(2 * tokens, tokens), :] = chosen
+    load.wait()
 
     def scatter(left, phase, out, into):
         for j in range(0, chunks, 2):
@@ -131,7 +149,7 @@
             )
             flat[pl.ds(j, tokens, stride=pad), :] = part[:, :LANES]
             flat[pl.ds(j + 1, tokens, stride=pad), :] = part[:, LANES:]
-        out[...] = flat[...].astype(BF16).reshape(tokens, pad, LANES)
+        out[...] = flat[...].reshape(tokens, pad // 8, 8, LANES).astype(BF16)
         spread(
             phase, tokens, rep * per_dp + sec, token_device, my_token,
             lambda t: out.at[t], into.at[me],
@@ -139,8 +157,10 @@
 
     def total(into):
         return lax.fori_loop(
-            0, devices, lambda n, acc: acc + into[n].astype(F32), jnp.zeros((pad, LANES), F32)
-        )
+            0, devices, lambda n, acc: acc + into[n].astype(F32),
+            jnp.zeros((pad // 8, 8, LANES), F32),
+            unroll=4,
+        ).reshape(pad, LANES)
 
     def spread_rows(values):
         tok[...] = values
@@ -151,7 +171,7 @@
     def pack_row(values, out):
         for j in range(chunks):
             tok[j : j + 1, :] = values[0:1, j * LANES : (j + 1) * LANES]
-        out[...] = tok[...].astype(BF16)
+        out[...] = tok[...].reshape(pad // 8, 8, LANES).astype(BF16)
 
     def norm(x):
         scale = lax.rsqrt(jnp.sum(x * x, axis=1, keepdims=True) * (1.0 / dim) + EPS)
@@ -159,11 +179,13 @@
 
     def weights(layer):
         s, c = layer % sections, layer // sections
-        return (
-            spread_rows(gains[s, c].astype(F32)),
-            wins[s, c].astype(F32),
-            wouts[s, c].astype(F32),
-        )
+        at = (s % 2, s // 2, c, 0)
+        return gain_wide[layer], wins[at].astype(F32), wouts[at].astype(F32)
+
+    def widen(layer, _):
+        s, c = layer % sections, layer // sections
+        gain_wide[layer] = spread_rows(gains[s % 2, s // 2, c].astype(F32).reshape(pad, LANES))
+        return 0
 
     def gather(phase, block, into):
         if_own(
@@ -173,16 +195,26 @@
         )
 
     def unpack(into, out):
-        flat[...] = into[...].reshape(tokens * pad, LANES).astype(F32)
+        flat[...] = into[...].astype(F32).reshape(tokens * pad, LANES)
         for j in range(chunks):
-            out[:, j * LANES : (j + 1) * LANES] = flat[
-                pl.ds(j, tokens, stride=pad), :
-            ].astype(BF16)
+            out(slice(j * LANES, (j + 1) * LANES), flat[pl.ds(j, tokens, stride=pad), :])
 
     scatter(chosen, LOOK, look_out, look_in)
-    take(gains, recv_sem.at[GAIN])
-    take(wins, recv_sem.at[WIN])
-    take(wouts, recv_sem.at[WOUT])
+    for phase, _, buf in stores:
+        take(buf.at[side], recv_sem.at[phase])
+        pltpu.make_async_remote_copy(
+            src_ref=buf.at[side],
+            dst_ref=buf.at[side],
+            send_sem=send_sem.at[phase + RELAY],
+            recv_sem=recv_sem.at[phase + RELAY],
+            device_id=(partner, rep),
+            device_id_type=pl.DeviceIdType.MESH,
+        ).start()
+    gain_wide[layers] = spread_rows(gain_ref[2].astype(F32).reshape(pad, LANES))
+    take(gains.at[1 - side], recv_sem.at[GAIN + RELAY])
+    lax.fori_loop(0, layers, widen, 0)
+    for phase, _, buf in stores[1:]:
+        take(buf.at[1 - side], recv_sem.at[phase + RELAY])
 
     def forward():
         take(look_in, recv_sem.at[LOOK])
@@ -191,20 +223,26 @@
         def layer(index, x):
             layer_in[index] = x
             gain, first, second = weights(index)
-            normed, _ = norm(x)
+            normed, scale = norm(x)
             pre = jnp.sum(rounded(normed * gain) * first, axis=1, keepdims=True)
             hidden = rounded(gelu_tanh(pre))
+            kept[index, 0] = jnp.broadcast_to(scale, (8, LANES))
+            kept[index, 1] = jnp.broadcast_to(gelu_slope(pre), (8, LANES))
             return rounded(x + jnp.sum(hidden * second, axis=0, keepdims=True))
 
         x = lax.fori_loop(0, layers, layer, x)
         layer_in[layers] = x
         normed, _ = norm(x)
-        pack_row(normed * spread_rows(fgain_ref[...].astype(F32)), head_out)
+        pack_row(normed * gain_wide[layers], head_out)
 
     if_own(forward)
     gather(HEAD, head_out, head_in)
     take(head_in, recv_sem.at[HEAD])
-    unpack(head_in, head_ref)
+
+    def store_head(lanes, part):
+        right_ref[pl.ds(0, tokens), lanes] = part.astype(BF16)
+
+    unpack(head_in, store_head)
 
     scores = lax.dot_general(
         head_ref[...], table_ref[...], (((1,), (1,)), ((), ())), preferred_element_type=F32
@@ -241,12 +279,12 @@
     score_grad = (
         (powers / wide(exp_total) - jnp.where(mask, 1.0, 0.0)) * (1.0 - squash * squash)
     ).astype(BF16)
-    sg_ref[...] = score_grad
+    left_ref[pl.ds(0, tokens), :] = score_grad
     scatter(score_grad, GRAD, grad_out, grad_in)
 
     def backward():
         take(grad_in, recv_sem.at[GRAD])
-        grad = spread_rows(total(grad_in)) * spread_rows(fgain_ref[...].astype(F32))
+        grad = spread_rows(total(grad_in)) * gain_wide[layers]
 
         def back(normed, scale, grad):
             mean = jnp.sum(grad * normed, axis=1, keepdims=True) * (1.0 / dim)
@@ -257,10 +295,10 @@
         def layer(step, dy):
             index = layers - 1 - step
             gain, first, second = weights(index)
-            normed, scale = norm(layer_in[index])
-            pre = jnp.sum(rounded(normed * gain) * first, axis=1, keepdims=True)
+            scale = kept[index, 0][:, 0:1]
+            normed = layer_in[index] * scale
             hidden_grad = jnp.sum(dy * second, axis=1, keepdims=True)
-            pre_grad = rounded(hidden_grad * gelu_slope(pre))
+            pre_grad = rounded(hidden_grad * kept[index, 1][:, 0:1])
             act_grad = jnp.sum(pre_grad * first, axis=0, keepdims=True)
             return rounded(dy + back(normed, scale, act_grad * gain))
 
@@ -269,11 +307,20 @@
     if_own(backward)
     gather(EMB, emb_out, emb_in)
     take(emb_in, recv_sem.at[EMB])
-    unpack(emb_in, emb_ref)
+
+    def store_emb(lanes, part):
+        part = part * scale_in
+        high = part.astype(BF16)
+        right_ref[pl.ds(tokens, tokens), lanes] = high
+        right_ref[pl.ds(2 * tokens, tokens), lanes] = (part - high.astype(F32)).astype(BF16)
+
+    unpack(emb_in, store_emb)
 
     take(idbuf.at[pl.ds(0, replicas - 1)], send_sem.at[IDS])
-    for phase, buf in ((GAIN, gains), (WIN, wins), (WOUT, wouts)):
-        take(buf.at[pl.ds(0, sections - 1)], send_sem.at[phase])
+    for phase, _, buf in stores:
+        if half > 1:
+            take(buf.at[0, pl.ds(0, half - 1)], send_sem.at[phase])
+        take(buf.at[0], send_sem.at[phase + RELAY])
     take(stat_in.at[pl.ds(0, devices - 1)], send_sem.at[STAT])
 
     def owned():
@@ -291,11 +338,11 @@
             take(grad_out, send_sem.at[GRAD])
 
 
-def table_kernel(scale, sg_ref, chosen_ref, head_ref, emb_ref, out_ref):
+def table_kernel(left_ref, right_ref, out_ref):
     over = (((0,), (0,)), ((), ()))
-    head = lax.dot_general(sg_ref[...], head_ref[...], over, preferred_element_type=F32)
-    emb = lax.dot_general(chosen_ref[...], emb_ref[...], over, preferred_element_type=F32)
-    out_ref[...] = (head + emb * scale).astype(BF16)
+    out_ref[...] = lax.dot_general(
+        left_ref[...], right_ref[...], over, preferred_element_type=F32
+    ).astype(BF16)
 
 
 def per_device(token_ids, target_ids, table, norm_gain, w_in, w_out, final_gain):
@@ -307,38 +354,37 @@
     tokens = replicas * per_dp
     devices = sections * replicas
     chunks = dim // LANES
-    pad = (chunks + 15) // 16 * 16
+    pad = (chunks + 7) // 8 * 8
     assert per_dp <= sections and tokens % 8 == 0
     assert chunks % 2 == 0 and rows_dev % LANES == 0
     ids = jnp.concatenate([token_ids.reshape(per_dp), target_ids.reshape(per_dp)])
     ids = jnp.broadcast_to(ids[:, None], (2 * per_dp, LANES))
-    fill = lambda rows: jnp.pad(
-        rows.reshape(rows.shape[:-1] + (chunks, LANES)),
-        ((0, 0),) * (rows.ndim - 1) + ((0, pad - chunks), (0, 0)),
+    gain_rows = jnp.concatenate([norm_gain[:, 0], final_gain[None]])
+    gain_rows = jnp.pad(gain_rows, ((0, 0), (0, pad * LANES - dim))).reshape(
+        3, pad // 8, 8, LANES
     )
-    block = (pad, LANES)
+    block = (pad // 8, 8, LANES)
     vmem = pl.BlockSpec(memory_space=pltpu.VMEM)
-    loss, score_grad, chosen, head, emb = pl.pallas_call(
+    anywhere = pl.BlockSpec(memory_space=pl.ANY)
+    loss, left, right = pl.pallas_call(
         functools.partial(cascade, sections, replicas, per_dp, pad),
         out_shape=(
             jax.ShapeDtypeStruct((tokens, LANES), F32),
-            jax.ShapeDtypeStruct((tokens, rows_dev), BF16),
-            jax.ShapeDtypeStruct((tokens, rows_dev), BF16),
-            jax.ShapeDtypeStruct((tokens, dim), BF16),
-            jax.ShapeDtypeStruct((tokens, dim), BF16),
+            jax.ShapeDtypeStruct((3 * tokens, rows_dev), BF16),
+            jax.ShapeDtypeStruct((3 * tokens, dim), BF16),
         ),
-        in_specs=[vmem] * 6,
-        out_specs=(vmem,) * 5,
+        in_specs=[vmem, anywhere, vmem, anywhere, anywhere],
+        out_specs=(vmem,) * 3,
         scratch_shapes=[
             pltpu.VMEM((replicas, 2 * per_dp, LANES), jnp.int32),
             pltpu.VMEM((2, tokens, LANES), jnp.int32),
-            pltpu.VMEM((sections, 2) + block, BF16),
-            pltpu.VMEM((sections, 2, rank, dim), BF16),
-            pltpu.VMEM((sections, 2, rank, dim), BF16),
+            pltpu.VMEM((2, sections // 2, 3) + block, BF16),
+            pltpu.VMEM((2, sections // 2, 2, 1, rank, dim), BF16),
+            pltpu.VMEM((2, sections // 2, 2, 1, rank, dim), BF16),
             pltpu.VMEM((tokens * pad, LANES), F32),
             pltpu.VMEM((tokens,) + block, BF16),
             pltpu.VMEM((devices,) + block, BF16),
-            pltpu.VMEM(block, F32),
+            pltpu.VMEM((pad, LANES), F32),
             pltpu.VMEM((2 * sections + 1, 8, dim), F32),
             pltpu.VMEM(block, BF16),
             pltpu.VMEM((tokens,) + block, BF16),
@@ -348,25 +394,29 @@
             pltpu.VMEM((devices,) + block, BF16),
             pltpu.VMEM(block, BF16),
             pltpu.VMEM((tokens,) + block, BF16),
-            pltpu.SemaphoreType.DMA((9,)),
-            pltpu.SemaphoreType.DMA((9,)),
+            pltpu.VMEM((rows_dev, dim), BF16),
+            pltpu.VMEM((2 * sections + 1, 8, dim), F32),
+            pltpu.VMEM((2 * sections, 2, 8, LANES), F32),
+            pltpu.SemaphoreType.DMA((13,)),
+            pltpu.SemaphoreType.DMA((13,)),
         ],
         compiler_params=pltpu.CompilerParams(
             collective_id=0, has_side_effects=True, vmem_limit_bytes=52 << 20
         ),
         name="cascade",
-    )(ids, table, fill(norm_gain[:, 0]), w_in[:, 0], w_out[:, 0], fill(final_gain))
-    step = 512
-    full = pl.BlockSpec((tokens, rows_dev), lambda i: (0, 0))
-    piece = pl.BlockSpec((tokens, step), lambda i: (0, i))
+    )(ids, table, gain_rows, w_in, w_out)
+    step = dim // 3
     table_grad = pl.pallas_call(
-        functools.partial(table_kernel, math.sqrt(dim)),
+        table_kernel,
         out_shape=jax.ShapeDtypeStruct((rows_dev, dim), BF16),
         grid=(dim // step,),
-        in_specs=[full, full, piece, piece],
+        in_specs=[
+            pl.BlockSpec((3 * tokens, rows_dev), lambda i: (0, 0)),
+            pl.BlockSpec((3 * tokens, step), lambda i: (0, i)),
+        ],
         out_specs=pl.BlockSpec((rows_dev, step), lambda i: (0, i)),
         name="table_grad",
-    )(score_grad, chosen, head, emb)
+    )(left, right)
     token_loss = lax.dynamic_slice_in_dim(
         loss[:, 0], lax.axis_index("dp") * per_dp, per_dp, 0
     ).reshape(batches, width)

time: 90.3 us -> 73.6 us (0.82)
  Pallas kernels: 80.4 us -> 65.3 us
  local copies, waits for them, and re-layouts: 8.24 us -> 6.42 us
    pallas_call x1, Pallas kernels: 73.8 us -> 61.5 us  [per_device(): pl.pallas_call(functools.partial(cascade, sections, replicas, per_dp, pad...]
    pallas_call x1, Pallas kernels: 6.66 us -> 3.8 us  [per_device(): pl.pallas_call(table_kernel, out_shape=jax.ShapeDtypeStruct((rows_dev, di...]
    unnamed x12 -> x9, local copies, waits for them, and re-layouts: 4.43 us -> 3.35 us
where the time goes in v2:
time: 73.6 us; the launch traced here: 73.2 us
  Pallas kernels  65.3 us (89%)
  local copies, waits for them, and re-layouts  6.42 us (9%)
  other arithmetic  0.85 us (1%)
    pallas_call x1, Pallas kernels, per_device(): pl.pallas_call(functools.partial(cascade, sections, replicas, per_dp, pad...  61.5 us
    pallas_call x1, Pallas kernels, per_device(): pl.pallas_call(table_kernel, out_shape=jax.ShapeDtypeStruct((rows_dev, di...  3.8 us
    unnamed x9, local copies, waits for them, and re-layouts  3.35 us

profile of v2, /device:TPU:0, one launch (start us, length us, event | category | flops | bytes accessed | tf_op | source)
XLA Modules:
  0.0 73.2 jit_solution(17571352101818120855)
XLA Ops:
  0.6 0.8 %reshape.19 = s32[4]{0:T(128)S(1)} reshape(s32[2,2]{1,0:T(2,128)} %param.7) | data formatting | bytes 32 | tf_op jit(solution)/shard_map/reshape | solution.py:360
  1.4 0.8 %reshape.20 = s32[4]{0:T(128)S(1)} reshape(s32[2,2]{1,0:T(2,128)} %param.8) | data formatting | bytes 32 | tf_op jit(solution)/shard_map/reshape | solution.py:360
  2.2 0.1 pad_add_fusion
  2.2 0.1 broadcast_in_dim.4.ids_ref
  2.3 0.7 broadcast_in_dim.10
  3.0 0.8 %fusion.3 = bf16[1,3,40,128]{3,1,2,0:T(4,128)(2,1)S(1)} fusion(bf16[1,4608]{1,0:T(2,128)(2,1)S(1)} %broadcast_in_dim.10, bf16[2,4608]{1,0:T(2,128)(2,1)} %bitcast.10), kind=kLoop, calls=%fused_computation.4 | loop fusion | flops 107520 | bytes 58368
  3.8 0.0 copy-start.1
  3.8 0.9 %copy-done.1 = bf16[2,1,8,4608]{3,2,1,0:T(8,128)(2,1)S(1)} copy-done((bf16[2,1,8,4608]{3,2,1,0:T(8,128)(2,1)S(1)}, bf16[2,1,8,4608]{3,2,1,0:T(8,128)(2,1)}, u32[]{:S(2)}) %copy-start.1) | copy-done | bytes 147480
  4.7 0.0 copy-start.2
  4.7 0.9 %copy-done.2 = bf16[2,1,8,4608]{3,2,1,0:T(8,128)(2,1)S(1)} copy-done((bf16[2,1,8,4608]{3,2,1,0:T(8,128)(2,1)S(1)}, bf16[2,1,8,4608]{3,2,1,0:T(8,128)(2,1)}, u32[]{:S(2)}) %copy-start.2) | copy-done | bytes 147480
  5.6 61.5 %cascade.1 = (f32[32,128]{1,0:T(8,128)S(1)}, bf16[96,256]{1,0:T(8,128)(2,1)S(1)}, bf16[96,4608]{1,0:T(8,128)(2,1)S(1)}) custom-call(s32[8,128]{1,0:T(8,128)S(1)} %broadcast_in_dim.4.ids_ref, bf16[256,4608]{1,0:T(8,128)(2,1)} %table_hbm.1, bf16[3,5,8,128]{3,2,1,0:T(8,128)(2,1)S(1)} %bitcast.8, bf16[2,1,8,4608]{3,2,1,0:T(8,128)(2,1)S(1)} %copy-done.1, ...), custom_call_target="tpu_custom_call" | custom-call | tf_op jit(solution)/shard_map/cascade/pallas_call | solution.py:369
  67.1 0.0 copy-start
  67.1 0.9 %copy-done = bf16[96,4608]{1,0:T(8,128)(2,1)} copy-done((bf16[96,4608]{1,0:T(8,128)(2,1)}, bf16[96,4608]{1,0:T(8,128)(2,1)S(1)}, u32[]{:S(2)}) %copy-start) | copy-done | bytes 884760
  68.1 0.0 copy-start.3
  68.1 0.6 copy-done.3
  68.7 0.1 dynamic-slice_reduce_fusion
  68.8 0.6 reshape.22
  69.4 3.8 %table_grad.1 = bf16[256,4608]{1,0:T(8,128)(2,1)} custom-call(bf16[96,256]{1,0:T(8,128)(2,1)} %copy-done.3, bf16[96,4608]{1,0:T(8,128)(2,1)} %copy-done), custom_call_target="tpu_custom_call" | custom-call | tf_op jit(solution)/shard_map/table_grad/pallas_call | solution.py:409
  (1 shorter events, 0.0 us)
Async XLA Ops:
  3.8 0.9 %copy-start.1 = (bf16[2,1,8,4608]{3,2,1,0:T(8,128)(2,1)S(1)}, bf16[2,1,8,4608]{3,2,1,0:T(8,128)(2,1)}, u32[]{:S(2)}) copy-start(bf16[2,1,8,4608]{3,2,1,0:T(8,128)(2,1)} %win_ref.1) | copy-start | bytes 442372
  4.7 0.9 %copy-start.2 = (bf16[2,1,8,4608]{3,2,1,0:T(8,128)(2,1)S(1)}, bf16[2,1,8,4608]{3,2,1,0:T(8,128)(2,1)}, u32[]{:S(2)}) copy-start(bf16[2,1,8,4608]{3,2,1,0:T(8,128)(2,1)} %wout_ref.1) | copy-start | bytes 442372
  67.1 0.9 %copy-start = (bf16[96,4608]{1,0:T(8,128)(2,1)}, bf16[96,4608]{1,0:T(8,128)(2,1)S(1)}, u32[]{:S(2)}) copy-start(bf16[96,4608]{1,0:T(8,128)(2,1)S(1)} %get-tuple-element.7.right_ref) | copy-start | bytes 2654212
  68.1 0.6 copy-start.3

commit v3 on v2

--- a/solution.py
+++ b/solution.py
@@ -17,6 +17,7 @@
 IDS, LOOK, HEAD, STAT, GRAD, EMB, GAIN, WIN, WOUT = range(9)
 RELAY = 3
 TABLE = 12
+PAIR = 13
 
 
 def gelu_tanh(values):
@@ -36,11 +37,11 @@
 
 def cascade(
     sections, replicas, per_dp, pad,
-    ids_ref, table_hbm, gain_ref, win_ref, wout_ref,
+    token_ref, target_ref, table_hbm, gain_ref, fgain_ref, win_ref, wout_ref,
     loss_ref, left_ref, right_ref,
-    idbuf, idrow, gains, wins, wouts, flat, look_out, look_in, tok, layer_in,
+    loss_all, ids_ref, idbuf, idrow, gains, wins, wouts, flat, look_out, look_in, tok, layer_in,
     head_out, head_in, stat_out, stat_in, grad_out, grad_in, emb_out, emb_in,
-    table_ref, gain_wide, kept, send_sem, recv_sem,
+    table_ref, gain_wide, kept, look_pair, grad_pair, send_sem, recv_sem,
 ):
     devices = sections * replicas
     tokens = replicas * per_dp
@@ -54,7 +55,13 @@
     offset = me * rows_dev
     all_own = per_dp == sections
     own = sec < per_dp
-    my_token = rep * per_dp + sec if all_own else jnp.where(own, rep * per_dp + sec, -1)
+    own_half = per_dp // 2
+    count_half = tokens // 2
+    half = sections // 2
+    side, partner = sec % 2, sec + 1 - 2 * (sec % 2)
+    my_half = rep * own_half + sec // 2
+    if not all_own:
+        my_half = jnp.where(own, my_half, -1)
 
     def if_own(body):
         if all_own:
@@ -83,7 +90,7 @@
 
             return 0
 
-        lax.fori_loop(0, count, step, 0, unroll=4)
+        lax.fori_loop(0, count, step, 0, unroll=8)
 
     def take(ref, sem):
         pltpu.make_async_copy(ref, ref, sem).wait()
@@ -91,8 +98,23 @@
     def any_device(n):
         return (n // replicas, n % replicas)
 
-    def token_device(t):
-        return (t % per_dp, t // per_dp)
+    def token_device(h):
+        return (2 * (h % own_half) + side, h // own_half)
+
+    def side_device(q):
+        return (2 * (q // replicas) + side, q % replicas)
+
+    side_me = (sec // 2) * replicas + rep
+
+    def pair_copy(phase, src, dst):
+        return pltpu.make_async_remote_copy(
+            src_ref=src,
+            dst_ref=dst,
+            send_sem=send_sem.at[phase],
+            recv_sem=recv_sem.at[phase],
+            device_id=(partner, rep),
+            device_id_type=pl.DeviceIdType.MESH,
+        )
 
     load = pltpu.make_async_copy(table_hbm, table_ref, recv_sem.at[TABLE])
     load.start()
@@ -105,14 +127,21 @@
         )
         return 0
 
-    lax.fori_loop(0, devices - 1, greet, 0)
+    lax.fori_loop(0, devices - 1, greet, 0, unroll=8)
     flat[...] = jnp.zeros_like(flat)
     tok[...] = jnp.zeros_like(tok)
+    row = lax.broadcasted_iota(jnp.int32, (2 * per_dp, LANES), 0)
+    made = jnp.zeros((2 * per_dp, LANES), jnp.int32)
+    batches, width = token_ref.shape
+    for b in range(batches):
+        for w in range(width):
+            k = b * width + w
+            made = jnp.where(row == k, token_ref[b : b + 1, w : w + 1], made)
+            made = jnp.where(row == per_dp + k, target_ref[b : b + 1, w : w + 1], made)
+    ids_ref[...] = made
     pl.semaphore_wait(barrier, devices - 1)
 
     spread(IDS, replicas, rep, lambda d: (sec, d), rep, lambda d: ids_ref, idbuf.at[rep])
-    half = sections // 2
-    side, partner = sec % 2, sec + 1 - 2 * (sec % 2)
     stores = ((GAIN, gain_ref, gains), (WIN, win_ref, wins), (WOUT, wout_ref, wouts))
     for phase, src, dst in stores:
         for i in range(1, half):
@@ -131,7 +160,8 @@
     for d in range(replicas):
         for kind in range(2):
             for k in range(per_dp):
-                idrow[kind, pl.ds(d * per_dp + k, 1), :] = idbuf[
+                at = (k % 2) * count_half + d * own_half + k // 2
+                idrow[kind, pl.ds(at, 1), :] = idbuf[
                     d, pl.ds(kind * per_dp + k, 1), :
                 ]
     wide = lambda value: jnp.concatenate([value] * (rows_dev // LANES), axis=1)
@@ -142,22 +172,29 @@
     left_ref[pl.ds(2 * tokens, tokens), :] = chosen
     load.wait()
 
-    def scatter(left, phase, out, into):
+    def scatter(left, phase, out, pair, into):
         for j in range(0, chunks, 2):
             part = jnp.dot(
                 left, table_ref[:, j * LANES : (j + 2) * LANES], preferred_element_type=F32
             )
             flat[pl.ds(j, tokens, stride=pad), :] = part[:, :LANES]
             flat[pl.ds(j + 1, tokens, stride=pad), :] = part[:, LANES:]
-        out[...] = flat[...].reshape(tokens, pad // 8, 8, LANES).astype(BF16)
+        mine = pl.ds(pl.multiple_of(side * (count_half * pad), 8), count_half * pad)
+        away = pl.ds(pl.multiple_of((1 - side) * (count_half * pad), 8), count_half * pad)
+        blocks = (count_half, pad // 8, 8, LANES)
+        out[1 - side] = flat[away, :].reshape(blocks).astype(BF16)
+        swap = pair_copy(phase + PAIR, out.at[1 - side], pair)
+        swap.start()
+        swap.wait()
+        out[side] = (flat[mine, :].reshape(blocks) + pair[...].astype(F32)).astype(BF16)
         spread(
-            phase, tokens, rep * per_dp + sec, token_device, my_token,
-            lambda t: out.at[t], into.at[me],
+            phase, count_half, rep * own_half + sec // 2, token_device, my_half,
+            lambda h: out.at[side, h], into.at[side_me],
         )
 
     def total(into):
         return lax.fori_loop(
-            0, devices, lambda n, acc: acc + into[n].astype(F32),
+            0, devices // 2, lambda n, acc: acc + into[n].astype(F32),
             jnp.zeros((pad // 8, 8, LANES), F32),
             unroll=4,
         ).reshape(pad, LANES)
@@ -184,22 +221,29 @@
 
     def widen(layer, _):
         s, c = layer % sections, layer // sections
-        gain_wide[layer] = spread_rows(gains[s % 2, s // 2, c].astype(F32).reshape(pad, LANES))
+        both = gains[s % 2, s // 2].astype(F32)
+        picked = jnp.where(c == 0, both[0:1], both[1:2])
+        gain_wide[layer] = jnp.broadcast_to(picked, (8, dim))
         return 0
 
     def gather(phase, block, into):
         if_own(
             lambda: spread(
-                phase, devices, me, any_device, me, lambda n: block, into.at[my_token]
+                phase, devices // 2, side_me, side_device, side_me,
+                lambda n: block, into.at[side, my_half],
             )
         )
+        take(into.at[side], recv_sem.at[phase])
+        relay = pair_copy(phase + PAIR, into.at[side], into.at[side])
+        relay.start()
+        relay.wait()
 
     def unpack(into, out):
         flat[...] = into[...].astype(F32).reshape(tokens * pad, LANES)
         for j in range(chunks):
             out(slice(j * LANES, (j + 1) * LANES), flat[pl.ds(j, tokens, stride=pad), :])
 
-    scatter(chosen, LOOK, look_out, look_in)
+    scatter(chosen, LOOK, look_out, look_pair, look_in)
     for phase, _, buf in stores:
         take(buf.at[side], recv_sem.at[phase])
         pltpu.make_async_remote_copy(
@@ -210,7 +254,7 @@
             device_id=(partner, rep),
             device_id_type=pl.DeviceIdType.MESH,
         ).start()
-    gain_wide[layers] = spread_rows(gain_ref[2].astype(F32).reshape(pad, LANES))
+    gain_wide[layers] = jnp.broadcast_to(fgain_ref[...].astype(F32), (8, dim))
     take(gains.at[1 - side], recv_sem.at[GAIN + RELAY])
     lax.fori_loop(0, layers, widen, 0)
     for phase, _, buf in stores[1:]:
@@ -237,7 +281,6 @@
 
     if_own(forward)
     gather(HEAD, head_out, head_in)
-    take(head_in, recv_sem.at[HEAD])
 
     def store_head(lanes, part):
         right_ref[pl.ds(0, tokens), lanes] = part.astype(BF16)
@@ -275,12 +318,17 @@
         )
 
     exp_total = column_of(0)
-    loss_ref[...] = jnp.log(exp_total) - column_of(groups)
+    loss_all[...] = jnp.log(exp_total) - column_of(groups)
+    for b in range(batches):
+        for w in range(width):
+            k = b * width + w
+            at = (k % 2) * count_half + rep * own_half + k // 2
+            loss_ref[b : b + 1, w : w + 1] = loss_all[pl.ds(at, 1), 0:1]
     score_grad = (
         (powers / wide(exp_total) - jnp.where(mask, 1.0, 0.0)) * (1.0 - squash * squash)
     ).astype(BF16)
     left_ref[pl.ds(0, tokens), :] = score_grad
-    scatter(score_grad, GRAD, grad_out, grad_in)
+    scatter(score_grad, GRAD, grad_out, grad_pair, grad_in)
 
     def backward():
         take(grad_in, recv_sem.at[GRAD])
@@ -306,7 +354,6 @@
 
     if_own(backward)
     gather(EMB, emb_out, emb_in)
-    take(emb_in, recv_sem.at[EMB])
 
     def store_emb(lanes, part):
         part = part * scale_in
@@ -324,24 +371,26 @@
     take(stat_in.at[pl.ds(0, devices - 1)], send_sem.at[STAT])
 
     def owned():
-        take(look_out.at[pl.ds(0, tokens - 1)], send_sem.at[LOOK])
-        take(grad_out.at[pl.ds(0, tokens - 1)], send_sem.at[GRAD])
-        take(look_in.at[pl.ds(0, devices - 1)], send_sem.at[HEAD])
-        take(grad_in.at[pl.ds(0, devices - 1)], send_sem.at[EMB])
+        take(look_pair.at[pl.ds(0, count_half - 1)], send_sem.at[LOOK])
+        take(grad_pair.at[pl.ds(0, count_half - 1)], send_sem.at[GRAD])
+        take(look_in.at[pl.ds(0, devices // 2 - 1)], send_sem.at[HEAD])
+        take(grad_in.at[pl.ds(0, devices // 2 - 1)], send_sem.at[EMB])
 
     if_own(owned)
     if not all_own:
 
         @pl.when(jnp.logical_not(own))
         def _():
-            take(look_out, send_sem.at[LOOK])
-            take(grad_out, send_sem.at[GRAD])
+            take(look_pair, send_sem.at[LOOK])
+            take(grad_pair, send_sem.at[GRAD])
 
 
 def table_kernel(left_ref, right_ref, out_ref):
     over = (((0,), (0,)), ((), ()))
+    step = out_ref.shape[1]
+    lanes = pl.ds(pl.multiple_of(pl.program_id(0) * step, LANES), step)
     out_ref[...] = lax.dot_general(
-        left_ref[...], right_ref[...], over, preferred_element_type=F32
+        left_ref[...], right_ref[:, lanes], over, preferred_element_type=F32
     ).astype(BF16)
 
 
@@ -357,69 +406,62 @@
     pad = (chunks + 7) // 8 * 8
     assert per_dp <= sections and tokens % 8 == 0
     assert chunks % 2 == 0 and rows_dev % LANES == 0
-    ids = jnp.concatenate([token_ids.reshape(per_dp), target_ids.reshape(per_dp)])
-    ids = jnp.broadcast_to(ids[:, None], (2 * per_dp, LANES))
-    gain_rows = jnp.concatenate([norm_gain[:, 0], final_gain[None]])
-    gain_rows = jnp.pad(gain_rows, ((0, 0), (0, pad * LANES - dim))).reshape(
-        3, pad // 8, 8, LANES
-    )
+    assert per_dp % 2 == 0 and sections % 2 == 0
     block = (pad // 8, 8, LANES)
     vmem = pl.BlockSpec(memory_space=pltpu.VMEM)
-    anywhere = pl.BlockSpec(memory_space=pl.ANY)
-    loss, left, right = pl.pallas_call(
+    hbm = pl.BlockSpec(memory_space=pltpu.HBM)
+    token_loss, left, right = pl.pallas_call(
         functools.partial(cascade, sections, replicas, per_dp, pad),
         out_shape=(
-            jax.ShapeDtypeStruct((tokens, LANES), F32),
+            jax.ShapeDtypeStruct((batches, width), F32),
             jax.ShapeDtypeStruct((3 * tokens, rows_dev), BF16),
             jax.ShapeDtypeStruct((3 * tokens, dim), BF16),
         ),
-        in_specs=[vmem, anywhere, vmem, anywhere, anywhere],
+        in_specs=[vmem, vmem, hbm, vmem, vmem, hbm, hbm],
         out_specs=(vmem,) * 3,
         scratch_shapes=[
+            pltpu.VMEM((tokens, LANES), F32),
+            pltpu.VMEM((2 * per_dp, LANES), jnp.int32),
             pltpu.VMEM((replicas, 2 * per_dp, LANES), jnp.int32),
             pltpu.VMEM((2, tokens, LANES), jnp.int32),
-            pltpu.VMEM((2, sections // 2, 3) + block, BF16),
+            pltpu.VMEM((2, sections // 2, 2, dim), BF16),
             pltpu.VMEM((2, sections // 2, 2, 1, rank, dim), BF16),
             pltpu.VMEM((2, sections // 2, 2, 1, rank, dim), BF16),
             pltpu.VMEM((tokens * pad, LANES), F32),
-            pltpu.VMEM((tokens,) + block, BF16),
-            pltpu.VMEM((devices,) + block, BF16),
+            pltpu.VMEM((2, tokens // 2) + block, BF16),
+            pltpu.VMEM((devices // 2,) + block, BF16),
             pltpu.VMEM((pad, LANES), F32),
             pltpu.VMEM((2 * sections + 1, 8, dim), F32),
             pltpu.VMEM(block, BF16),
-            pltpu.VMEM((tokens,) + block, BF16),
+            pltpu.VMEM((2, tokens // 2) + block, BF16),
             pltpu.VMEM((8, LANES), F32),
             pltpu.VMEM((devices, 8, LANES), F32),
-            pltpu.VMEM((tokens,) + block, BF16),
-            pltpu.VMEM((devices,) + block, BF16),
+            pltpu.VMEM((2, tokens // 2) + block, BF16),
+            pltpu.VMEM((devices // 2,) + block, BF16),
             pltpu.VMEM(block, BF16),
-            pltpu.VMEM((tokens,) + block, BF16),
+            pltpu.VMEM((2, tokens // 2) + block, BF16),
             pltpu.VMEM((rows_dev, dim), BF16),
             pltpu.VMEM((2 * sections + 1, 8, dim), F32),
             pltpu.VMEM((2 * sections, 2, 8, LANES), F32),
-            pltpu.SemaphoreType.DMA((13,)),
-            pltpu.SemaphoreType.DMA((13,)),
+            pltpu.VMEM((tokens // 2,) + block, BF16),
+            pltpu.VMEM((tokens // 2,) + block, BF16),
+            pltpu.SemaphoreType.DMA((19,)),
+            pltpu.SemaphoreType.DMA((19,)),
         ],
         compiler_params=pltpu.CompilerParams(
-            collective_id=0, has_side_effects=True, vmem_limit_bytes=52 << 20
+            collective_id=0, has_side_effects=True, vmem_limit_bytes=63400000
         ),
         name="cascade",
-    )(ids, table, gain_rows, w_in, w_out)
+    )(token_ids, target_ids, table, norm_gain[:, 0], final_gain[None], w_in, w_out)
     step = dim // 3
     table_grad = pl.pallas_call(
         table_kernel,
         out_shape=jax.ShapeDtypeStruct((rows_dev, dim), BF16),
         grid=(dim // step,),
-        in_specs=[
-            pl.BlockSpec((3 * tokens, rows_dev), lambda i: (0, 0)),
-            pl.BlockSpec((3 * tokens, step), lambda i: (0, i)),
-        ],
+        in_specs=[vmem, vmem],
         out_specs=pl.BlockSpec((rows_dev, step), lambda i: (0, i)),
         name="table_grad",
     )(left, right)
-    token_loss = lax.dynamic_slice_in_dim(
-        loss[:, 0], lax.axis_index("dp") * per_dp, per_dp, 0
-    ).reshape(batches, width)
     return (token_loss, table_grad)
 
 

time: 73.6 us -> 62.1 us (0.84)
  Pallas kernels: 65.3 us -> 59.3 us
  local copies, waits for them, and re-layouts: 6.42 us -> 1.89 us
  other arithmetic: 0.85 us -> 0 us
    pallas_call x1, Pallas kernels: 61.5 us -> 55.5 us  [per_device(): pl.pallas_call(functools.partial(cascade, sections, replicas, per_dp, pad...]
    unnamed x9 -> x3, local copies, waits for them, and re-layouts: 3.35 us -> 0.57 us
    reshape x3 -> x0, local copies, waits for them, and re-layouts: 2.17 us -> none  [the longest x1 0.76 us: per_device(): token_ids.reshape(per_dp)]
    unnamed x1 -> x0, other arithmetic: 0.77 us -> none
where the time goes in v3:
time: 62.1 us; the launch traced here: 61.8 us
  Pallas kernels  59.3 us (95%)
  local copies, waits for them, and re-layouts  1.89 us (3%)
  between operations  0.65 us (1%)
    pallas_call x1, Pallas kernels, per_device(): pl.pallas_call(functools.partial(cascade, sections, replicas, per_dp, pad...  55.5 us
    pallas_call x1, Pallas kernels, per_device(): pl.pallas_call(table_kernel, out_shape=jax.ShapeDtypeStruct((rows_dev, di...  3.75 us
    broadcast_in_dim x1, local copies, waits for them, and re-layouts, per_device(): final_gain[None]  1.32 us

profile of v3, /device:TPU:0, one launch (start us, length us, event | category | flops | bytes accessed | tf_op | source)
XLA Modules:
  0.0 61.8 jit_solution(14587767746915228550)
XLA Ops:
  0.6 1.3 %broadcast_in_dim.3.fgain_ref = bf16[1,4608]{1,0:T(2,128)(2,1)} reshape(bf16[4608]{0:T(1024)(128)(2,1)} %param.13) | data formatting | bytes 18432 | tf_op jit(solution)/shard_map/broadcast_in_dim | solution.py:455
  1.9 55.5 %cascade.1 = (f32[2,2]{1,0:T(2,128)}, bf16[96,256]{1,0:T(8,128)(2,1)}, bf16[96,4608]{1,0:T(8,128)(2,1)}) custom-call(s32[2,2]{1,0:T(2,128)} %token_ref.1, s32[2,2]{1,0:T(2,128)} %target_ref.1, bf16[256,4608]{1,0:T(8,128)(2,1)} %table_hbm.1, bf16[2,4608]{1,0:T(2,128)(2,1)} %bitcast.1, bf16[1,4608]{1,0:T(2,128)(2,1)} %broadcast_in_dim.3.fgain_ref, ...), custom_call_target="tpu_custom_call" | custom-call | tf_op jit(solution)/shard_map/cascade/pallas_call | solution.py:413
  57.5 0.0 copy-start
  57.5 3.8 %table_grad.1 = bf16[256,4608]{1,0:T(8,128)(2,1)} custom-call(bf16[96,256]{1,0:T(8,128)(2,1)} %get-tuple-element.6.left_ref, bf16[96,4608]{1,0:T(8,128)(2,1)} %get-tuple-element.7.right_ref), custom_call_target="tpu_custom_call" | custom-call | tf_op jit(solution)/shard_map/table_grad/pallas_call | solution.py:457
  61.3 0.0 copy-done
  61.3 0.6 copy.10
Async XLA Ops:
  57.5 3.8 %copy-start = (f32[2,2]{1,0:T(2,128)S(1)}, f32[2,2]{1,0:T(2,128)}, u32[]{:S(2)}) copy-start(f32[2,2]{1,0:T(2,128)} %get-tuple-element.10) | copy-start | bytes 52

commit v4 on v3

--- a/solution.py
+++ b/solution.py
@@ -254,7 +254,7 @@
             device_id=(partner, rep),
             device_id_type=pl.DeviceIdType.MESH,
         ).start()
-    gain_wide[layers] = jnp.broadcast_to(fgain_ref[...].astype(F32), (8, dim))
+    gain_wide[layers] = jnp.broadcast_to(fgain_ref[...].astype(F32)[None], (8, dim))
     take(gains.at[1 - side], recv_sem.at[GAIN + RELAY])
     lax.fori_loop(0, layers, widen, 0)
     for phase, _, buf in stores[1:]:
@@ -274,7 +274,7 @@
             kept[index, 1] = jnp.broadcast_to(gelu_slope(pre), (8, LANES))
             return rounded(x + jnp.sum(hidden * second, axis=0, keepdims=True))
 
-        x = lax.fori_loop(0, layers, layer, x)
+        x = lax.fori_loop(0, layers, layer, x, unroll=2)
         layer_in[layers] = x
         normed, _ = norm(x)
         pack_row(normed * gain_wide[layers], head_out)
@@ -350,7 +350,7 @@
             act_grad = jnp.sum(pre_grad * first, axis=0, keepdims=True)
             return rounded(dy + back(normed, scale, act_grad * gain))
 
-        pack_row(lax.fori_loop(0, layers, layer, dy), emb_out)
+        pack_row(lax.fori_loop(0, layers, layer, dy, unroll=2), emb_out)
 
     if_own(backward)
     gather(EMB, emb_out, emb_in)
@@ -452,7 +452,7 @@
             collective_id=0, has_side_effects=True, vmem_limit_bytes=63400000
         ),
         name="cascade",
-    )(token_ids, target_ids, table, norm_gain[:, 0], final_gain[None], w_in, w_out)
+    )(token_ids, target_ids, table, norm_gain[:, 0], final_gain, w_in, w_out)
     step = dim // 3
     table_grad = pl.pallas_call(
         table_kernel,

time: 62.1 us -> 60.5 us (0.974)
  local copies, waits for them, and re-layouts: 1.89 us -> 0.57 us
    broadcast_in_dim x1 -> x0, local copies, waits for them, and re-layouts: 1.32 us -> none  [per_device(): final_gain[None]]
where the time goes in v4:
time: 60.5 us; the launch traced here: 60.3 us
  Pallas kernels  59.1 us (98%)
  between operations  0.65 us (1%)
    pallas_call x1, Pallas kernels, per_device(): pl.pallas_call(functools.partial(cascade, sections, replicas, per_dp, pad...  55.3 us
    pallas_call x1, Pallas kernels, per_device(): pl.pallas_call(table_kernel, out_shape=jax.ShapeDtypeStruct((rows_dev, di...  3.75 us

profile of v4, /device:TPU:0, one launch (start us, length us, event | category | flops | bytes accessed | tf_op | source)
XLA Modules:
  0.0 60.3 jit_solution(2380819048717648206)
XLA Ops:
  0.6 55.3 %cascade.1 = (f32[2,2]{1,0:T(2,128)}, bf16[96,256]{1,0:T(8,128)(2,1)}, bf16[96,4608]{1,0:T(8,128)(2,1)}) custom-call(s32[2,2]{1,0:T(2,128)} %token_ref.1, s32[2,2]{1,0:T(2,128)} %target_ref.1, bf16[256,4608]{1,0:T(8,128)(2,1)} %table_hbm.1, bf16[2,4608]{1,0:T(2,128)(2,1)} %bitcast.1, bf16[4608]{0:T(1024)(128)(2,1)} %fgain_ref.1, ...), custom_call_target="tpu_custom_call" | custom-call | tf_op jit(solution)/shard_map/cascade/pallas_call | solution.py:413
  56.0 0.0 copy-start
  56.0 3.8 %table_grad.1 = bf16[256,4608]{1,0:T(8,128)(2,1)} custom-call(bf16[96,256]{1,0:T(8,128)(2,1)} %get-tuple-element.6.left_ref, bf16[96,4608]{1,0:T(8,128)(2,1)} %get-tuple-element.7.right_ref), custom_call_target="tpu_custom_call" | custom-call | tf_op jit(solution)/shard_map/table_grad/pallas_call | solution.py:457
  59.8 0.0 copy-done
  59.8 0.6 copy.10
Async XLA Ops:
  56.0 3.8 %copy-start = (f32[2,2]{1,0:T(2,128)S(1)}, f32[2,2]{1,0:T(2,128)}, u32[]{:S(2)}) copy-start(f32[2,2]{1,0:T(2,128)} %get-tuple-element.10) | copy-start | bytes 52
